TPU v7x, 32 devices: a whole 2x2x4 slice. The times are simulated.
32 devices in a mesh: leaf: 8 (over z, y), rep: 4 (over x, core).
Axes of the slice: x: 2, y: 2, z: 4, core: 2. Of those that a mesh axis runs over, the one named last changes fastest.
Arguments:
- coords: float32 [8, 8192], P(None, 'leaf'), may hold values from -8 to 8
- skeleton: float32 [8, 1024], P(None, 'leaf'), may hold values from -8 to 8
- transfer: bfloat16 [16, 64, 64], P('leaf'), may hold values from -0.75 to 0.75
- coupling: bfloat16 [256, 256], replicated, may hold values from -3 to 3, as said below
- parent: int32 [16], P('leaf'), may hold values from 0 to 3, never falling along the last dimension, each value on 1 to 6 neighbouring positions
- near_mask: int32 [16, 5], P('leaf'), may hold values from 0 to 1, as said below
- noise: float32 [8192], P('leaf'), may hold values from 0.5 to 2
- rhs: float32 [64, 8192], P('rep', 'leaf'), may hold values from -5 to 5
Outputs:
- solution: float32 [64, 8192], P('rep', 'leaf')
- residual: float32 [64, 8192], P('rep', 'leaf')
Inputs may be any that keep to these rules, and one draw needn't show every extreme that they name: `coupling`: symmetric positive semidefinite. `parent`: never falling along the leaves. Slot 2 is 1; near_mask[l, 2 + o] = near_mask[l + o, 2 - o]; slots pointing before the first or after the last leaf are 0.
All inputs are finite; a program needn't handle non-finite values.
Results may differ from a plain program's by a relative error of at most 0.0003.
Values sent between devices are 32-bit elements; how exact they have to be, the bound alone decides.
A program may use at most 64 MiB of HBM per device.

v0:
```python
import functools
import math

import jax
import jax.numpy as jnp
from jax import lax
from jax.experimental import pallas as pl
from jax.experimental.pallas import tpu as pltpu
from jax.sharding import PartitionSpec as P

ITERS = 2
LENGTH_SCALE = 4.0
SCALE = math.sqrt(3.0) / LENGTH_SCALE
TILE = 256
KEEP_LOW = True
BF = jnp.bfloat16
F32 = jnp.float32
LANES = 128


def dot(a, b):
    return lax.dot_general(a, b, (((1,), (0,)), ((), ())), preferred_element_type=F32)


def dot_nt(a, b):
    return lax.dot_general(a, b, (((1,), (1,)), ((), ())), preferred_element_type=F32)


def split(x):
    high = x.astype(BF)
    return high, (x - high.astype(F32)).astype(BF)


def stacked(x):
    high = x.astype(BF).astype(F32)
    return jnp.concatenate([high, x - high], axis=0).astype(BF)


def folded(x):
    half = x.shape[0] // 2
    return x[:half] + x[half:]


def features(x):
    p = x * SCALE
    high = p.astype(BF).astype(F32)
    middle = (p - high).astype(BF).astype(F32)
    low = p - high - middle
    norm = jnp.sum(p * p, axis=0, keepdims=True)
    norm_high = norm.astype(BF).astype(F32)
    norm_middle = (norm - norm_high).astype(BF).astype(F32)
    norm_low = norm - norm_high - norm_middle
    row = lax.broadcasted_iota(jnp.int32, (8, x.shape[1]), 0)

    def norms(first):
        at = row - first
        return jnp.where(
            at == 0,
            norm_high,
            jnp.where(
                at == 1,
                norm_middle,
                jnp.where(at == 2, norm_low, jnp.where(row < 6, 1.0, 0.0)),
            ),
        )

    blank = jnp.zeros((8, x.shape[1]), F32)
    left = jnp.concatenate([high, middle, high, middle, low, high, norms(0), blank], axis=0)
    h2, m2, l2 = -2.0 * high, -2.0 * middle, -2.0 * low
    right = jnp.concatenate([h2, h2, m2, m2, h2, l2, norms(3), blank], axis=0)
    return left, right


def matern(left, right):
    squared = jnp.maximum(dot(left, right), 1e-30)
    s = squared * lax.rsqrt(squared)
    return (1.0 + s) * jnp.exp(-s)


def loop(count, body):
    if count <= 16:
        for i in range(count):
            body(i)
    else:
        lax.fori_loop(0, count, lambda i, c: (body(i), c)[1], 0)


def kernel(
    n,
    coords, skeleton, transfer, coupling, parent, near_mask, noise, rhs,
    solution_ref, residual_ref,
    halo_x, halo_v0, halo_v1, left_t, right_f, kept_high, kept_low,
    near_sum, moved, ut_high, ut_low, g_high, g_low,
    coef_out, coef_in, sum_out, sum_in,
    x_send, x_recv, v_send, v_recv, c_send, c_recv, i_send, i_recv,
):
    me = lax.axis_index("leaf")
    leaves, slots = near_mask.shape
    reach = slots // 2
    points = coords.shape[1]
    leaf = points // leaves
    rank = transfer.shape[1]
    wide = coupling.shape[0]
    count = rhs.shape[0]

    barrier = pltpu.get_barrier_semaphore()

    def greet(i):
        pl.semaphore_signal(
            barrier, inc=1, device_id={"leaf": lax.rem(me + i + 1, n)},
            device_id_type=pl.DeviceIdType.MESH,
        )

    loop(n - 1, greet)

    def copy(src, dst, send, recv, target):
        return pltpu.make_async_remote_copy(
            src_ref=src, dst_ref=dst, send_sem=send, recv_sem=recv,
            device_id={"leaf": target}, device_id_type=pl.DeviceIdType.MESH,
        )

    def halo(src, dst, send, recv):
        to_left = copy(src, dst.at[1], send.at[0], recv.at[1], jnp.maximum(me - 1, 0))
        to_right = copy(src, dst.at[0], send.at[1], recv.at[0], jnp.minimum(me + 1, n - 1))

        def start():
            pl.when(me > 0)(lambda: to_left.start())
            pl.when(me < n - 1)(lambda: to_right.start())

        def finish():
            @pl.when(me > 0)
            def _():
                to_left.wait_send()
                to_right.wait_recv()

            @pl.when(me < n - 1)
            def _():
                to_right.wait_send()
                to_left.wait_recv()

        return start, finish

    def spread(src, dst, send, recv):
        def one(i):
            return copy(src, dst.at[i], send.at[i], recv.at[i], lax.rem(me + i + 1, n))

        def start():
            loop(n - 1, lambda i: one(i).start())

        def finish():
            loop(n - 1, lambda i: one(i).wait())

        return start, finish

    def total(own, got):
        if n <= 16:
            value = own[...]
            for i in range(n - 1):
                value = value + got[i]
            return value
        return lax.fori_loop(0, n - 1, lambda i, s: s + got[i], own[...])

    @pl.when(me == 0)
    def _():
        for h in (halo_x, halo_v0, halo_v1):
            h[0] = jnp.zeros(h.shape[1:], F32)

    @pl.when(me == n - 1)
    def _():
        for h in (halo_x, halo_v0, halo_v1):
            h[1] = jnp.zeros(h.shape[1:], F32)

    pl.semaphore_wait(barrier, n - 1)
    start_x, finish_x = halo(coords, halo_x, x_send, x_recv)
    start_v, finish_v = halo(rhs, halo_v0, v_send.at[0], v_recv.at[0])
    start_x()
    start_v()

    left, right = features(coords[...])
    left_t[pl.ds(points, points)] = left.T.astype(BF)
    right_f[...] = right.astype(BF)

    skeleton_t = features(skeleton[...])[0].T.astype(BF)
    for l in range(leaves):
        across = pl.ds(l * leaf, leaf)
        bases_t = matern(skeleton_t[l * rank:(l + 1) * rank], right_f[:, across])
        b_high, b_low = split(bases_t * (1.0 / math.sqrt(leaf)))
        q = lax.broadcasted_iota(jnp.int32, (wide, rank), 0)
        s = lax.broadcasted_iota(jnp.int32, (wide, rank), 1)
        place = jnp.where(q == s + parent[l] * rank, 1.0, 0.0).astype(BF)
        placed = dot_nt(place, transfer[l]).astype(BF)
        ut = dot(placed, b_high) + dot(placed, b_low)
        u_high, u_low = split(ut)
        ut_high[:, across] = u_high
        ut_low[:, across] = u_low
        g = dot(coupling[...], u_high) + dot(coupling[...], u_low)
        g1, g2 = split(g)
        g_high[:, across] = g1
        g_low[:, across] = g2

    def far_up(v):
        both = stacked(v)
        return folded(dot_nt(both, ut_high[...])) + dot_nt(both[:count], ut_low[...])

    def far_down(s):
        both = stacked(s)
        image = folded(dot(both, coupling[...]))
        far = folded(dot(both, g_high[...])) + dot(both[:count], g_low[...])
        return image, far

    def row_sum(x):
        return jnp.sum(x, axis=1, keepdims=True)

    def send_coefs(it, v):
        coef_out[it, :, :wide] = far_up(v)
        coef_out[it, :, wide:] = jnp.broadcast_to(row_sum(v * v), (count, LANES))
        start, finish = spread(coef_out.at[it], coef_in.at[it], c_send.at[it], c_recv.at[it])
        start()
        return finish

    def near_block(l, t, first, columns):
        scale = near_mask[l, t].astype(F32) * (1.0 / leaf)
        across = slice(l * leaf, (l + 1) * leaf)
        acc = None
        for j in range(0, leaf, TILE):
            kept = pl.ds(t * leaf + j, TILE)
            if first:
                where = points + (l + t - reach) * leaf + j
                k = matern(left_t[where:where + TILE], right_f[:, across])
                k_high = k.astype(BF)
                kept_high[l, kept] = k_high
                if KEEP_LOW:
                    k_low = (k - k_high.astype(F32)).astype(BF)
                    kept_low[l, kept] = k_low
            else:
                k_high = kept_high[l, kept]
                if KEEP_LOW:
                    k_low = kept_low[l, kept]
            part = columns[:, j:j + TILE]
            term = folded(dot(part, k_high))
            if KEEP_LOW:
                term = term + dot(part[:count], k_low)
            acc = term if acc is None else acc + term
        near_sum[:, across] += scale * acc

    def near(first, v, halos, finish):
        near_sum[...] = jnp.zeros_like(near_sum)
        own = [], []
        for l in range(leaves):
            for t in range(slots):
                m = l + t - reach
                own[0 if 0 <= m < leaves else 1].append((l, t, m))
        both = stacked(v)
        for l, t, m in own[0]:
            near_block(l, t, first, both[:, m * leaf:(m + 1) * leaf])
        finish()
        if first:
            for side in range(2):
                far_left = features(halo_x[side])[0]
                left_t[pl.ds(2 * side * points, points)] = far_left.T.astype(BF)
        sides = [stacked(halos[0]), stacked(halos[1])]
        for l, t, m in own[1]:
            side = 0 if m < 0 else 1
            at = m + leaves if m < 0 else m - leaves
            near_block(l, t, first, sides[side][:, at * leaf:(at + 1) * leaf])
        diagonal = []
        for l in range(leaves):
            ones = near_mask[l, 0]
            for t in range(1, slots):
                ones = ones + near_mask[l, t]
            diagonal.append(noise[:, l * leaf:(l + 1) * leaf] + ones.astype(F32))
        return jnp.concatenate(diagonal, axis=1) * v + near_sum[...]

    def whole_pass(it, v, local, finish_c):
        sum_out[it] = jnp.broadcast_to(row_sum(v * local), (count, LANES))
        start, finish = spread(sum_out.at[it], sum_in.at[it], i_send.at[it], i_recv.at[it])
        start()
        finish_c()
        value = total(coef_out.at[it], coef_in.at[it])
        s, norm = value[:, :wide], value[:, wide:wide + 1]
        image, far = far_down(s)
        extra = row_sum(s * image)
        finish()
        inner = total(sum_out.at[it], sum_in.at[it])[:, :1] + extra
        return local + far, norm, inner

    r0 = rhs[...]
    finish_c = send_coefs(0, r0)

    def arrived():
        finish_x()
        finish_v()

    local = near(True, r0, halo_v0, arrived)
    applied0, norm0, inner0 = whole_pass(0, r0, local, finish_c)
    step0 = norm0 / inner0
    r1 = r0 - step0 * applied0
    moved[...] = r1
    solution_ref[...] = step0 * r0
    residual_ref[...] = applied0
    start_v, finish_v1 = halo(moved, halo_v1, v_send.at[1], v_recv.at[1])
    start_v()

    finish_c = send_coefs(1, r1)
    local = near(False, r1, halo_v1, finish_v1)
    applied1, norm1, inner1 = whole_pass(1, r1, local, finish_c)
    growth = norm1 / norm0
    step1 = norm1 / (inner1 - growth * norm1 / step0)
    solution_ref[...] = solution_ref[...] + step1 * (r1 + growth * rhs[...])
    residual_ref[...] = r1 - step1 * (applied1 + growth * residual_ref[...])


def per_device(coords, skeleton, transfer, coupling, parent, near_mask, noise, rhs):
    n = lax.axis_size("leaf")
    leaves, slots = near_mask.shape
    points = coords.shape[1]
    leaf = points // leaves
    wide = coupling.shape[0]
    count = rhs.shape[0]
    vmem = pl.BlockSpec(memory_space=pltpu.VMEM)
    smem = pl.BlockSpec(memory_space=pltpu.SMEM)
    peers = max(n - 1, 1)
    dma = pltpu.SemaphoreType.DMA
    return pl.pallas_call(
        functools.partial(kernel, n),
        out_shape=(jax.ShapeDtypeStruct(rhs.shape, F32),) * 2,
        in_specs=[vmem, vmem, vmem, vmem, smem, smem, vmem, vmem],
        out_specs=(vmem, vmem),
        scratch_shapes=[
            pltpu.VMEM((2,) + coords.shape, F32),
            pltpu.VMEM((2, count, points), F32),
            pltpu.VMEM((2, count, points), F32),
            pltpu.VMEM((3 * points, 64), BF),
            pltpu.VMEM((64, points), BF),
            pltpu.VMEM((leaves, slots * leaf, leaf), BF),
            pltpu.VMEM((leaves, slots * leaf, leaf) if KEEP_LOW else (1, 16, LANES), BF),
            pltpu.VMEM((count, points), F32),
            pltpu.VMEM((count, points), F32),
            pltpu.VMEM((wide, points), BF),
            pltpu.VMEM((wide, points), BF),
            pltpu.VMEM((wide, points), BF),
            pltpu.VMEM((wide, points), BF),
            pltpu.VMEM((ITERS, count, wide + LANES), F32),
            pltpu.VMEM((ITERS, peers, count, wide + LANES), F32),
            pltpu.VMEM((ITERS, count, LANES), F32),
            pltpu.VMEM((ITERS, peers, count, LANES), F32),
            dma((2,)), dma((2,)), dma((2, 2)), dma((2, 2)),
            dma((ITERS, peers)), dma((ITERS, peers)), dma((ITERS, peers)), dma((ITERS, peers)),
        ],
        compiler_params=pltpu.CompilerParams(
            collective_id=0, has_side_effects=True, vmem_limit_bytes=60 * 1024 * 1024
        ),
    )(coords, skeleton, transfer, coupling, parent, near_mask, noise.reshape(1, points), rhs)


def solution(mesh):
    return jax.shard_map(
        per_device,
        mesh=mesh,
        in_specs=(
            P(None, "leaf"),
            P(None, "leaf"),
            P("leaf", None, None),
            P(),
            P("leaf"),
            P("leaf", None),
            P("leaf"),
            P("rep", "leaf"),
        ),
        out_specs=(P("rep", "leaf"), P("rep", "leaf")),
        check_vma=False,
    )
```

profile of v0, /device:TPU:0, one launch (start us, length us, event | category | flops | bytes accessed | tf_op | source)
XLA Modules:
  0.0 36.1 jit_solution(17175310334443439293)
XLA Ops:
  0.6 33.3 %shard_map.95 = (f32[16,1024]{1,0:T(8,128)}, f32[16,1024]{1,0:T(8,128)}) custom-call(f32[8,1024]{1,0:T(8,128)} %coords.1, f32[8,128]{1,0:T(8,128)} %skeleton.1, bf16[2,64,64]{2,1,0:T(8,128)(2,1)} %transfer.1, bf16[256,256]{1,0:T(8,128)(2,1)} %coupling.1, s32[2]{0:T(128)} %parent.1, s32[2,5]{1,0:T(2,128)} %near_mask.1, f32[1,1024]{1,0:T(1,128)} %bitcast.1, ...), custom_call_target="tpu_custom_call" | custom-call | tf_op jit(solution)/shard_map/pallas_call | solution.py:324
  34.0 0.0 copy-start
  34.0 1.5 %copy.12 = f32[16,1024]{1,0:T(8,128)} copy(f32[16,1024]{1,0:T(8,128)} %get-tuple-element.4) | data formatting | bytes 131072
  35.5 0.0 copy-done
  35.5 0.6 %copy.13 = f32[16,1024]{1,0:T(8,128)} copy(f32[16,1024]{1,0:T(8,128)S(1)} %copy-done) | data formatting | bytes 131072
Async XLA Ops:
  34.0 1.5 %copy-start = (f32[16,1024]{1,0:T(8,128)S(1)}, f32[16,1024]{1,0:T(8,128)}, u32[]{:S(2)}) copy-start(f32[16,1024]{1,0:T(8,128)} %get-tuple-element.5) | copy-start | bytes 196612
where the time goes:
time: 36.3 us; the launch traced here: 36.1 us
  Pallas kernels  33.3 us (92%)
  local copies, waits for them, and re-layouts  2.14 us (6%)
  between operations  0.65 us (2%)
    pallas_call x1, Pallas kernels, per_device(): pl.pallas_call(functools.partial(kernel, n), out_shape=(jax.ShapeDtypeStr...  33.3 us
    unnamed x4, local copies, waits for them, and re-layouts  2.14 us

commit v1 on v0

--- a/solution.py
+++ b/solution.py
@@ -92,7 +92,7 @@
     halo_x, halo_v0, halo_v1, left_t, right_f, kept_high, kept_low,
     near_sum, moved, ut_high, ut_low, g_high, g_low,
     coef_out, coef_in, sum_out, sum_in,
-    x_send, x_recv, v_send, v_recv, c_send, c_recv, i_send, i_recv,
+    x_send, x_recv, v_send, v_recv, c_send, c_recv, i_send, i_recv, ready,
 ):
     me = lax.axis_index("leaf")
     leaves, slots = near_mask.shape
@@ -105,13 +105,26 @@
 
     barrier = pltpu.get_barrier_semaphore()
 
-    def greet(i):
+    def tell(sem, target):
         pl.semaphore_signal(
-            barrier, inc=1, device_id={"leaf": lax.rem(me + i + 1, n)},
-            device_id_type=pl.DeviceIdType.MESH,
+            sem, inc=1, device_id={"leaf": target}, device_id_type=pl.DeviceIdType.MESH
         )
 
-    loop(n - 1, greet)
+    stages = n.bit_length() - 1
+    partners = [me + 2**b * (1 - 2 * lax.rem(me // 2**b, 2)) for b in range(stages)]
+    other = me - 1 + 2 * lax.rem(me, 2)
+    has_other = jnp.logical_and(other >= 0, other < n)
+    for target in partners:
+        tell(barrier, target)
+    pl.when(has_other)(lambda: tell(barrier, other))
+
+    def stage(b):
+        def run():
+            if b > 0:
+                pl.semaphore_wait(ready.at[b - 1], 1)
+            if b < stages:
+                tell(ready.at[b], partners[b])
+        return run
 
     def copy(src, dst, send, recv, target):
         return pltpu.make_async_remote_copy(
@@ -170,7 +183,9 @@
         for h in (halo_x, halo_v0, halo_v1):
             h[1] = jnp.zeros(h.shape[1:], F32)
 
-    pl.semaphore_wait(barrier, n - 1)
+    pl.when(has_other)(lambda: pl.semaphore_wait(barrier, stages + 1))
+    pl.when(jnp.logical_not(has_other))(lambda: pl.semaphore_wait(barrier, stages))
+    stage(0)()
     start_x, finish_x = halo(coords, halo_x, x_send, x_recv)
     start_v, finish_v = halo(rhs, halo_v0, v_send.at[0], v_recv.at[0])
     start_x()
@@ -208,15 +223,21 @@
         far = folded(dot(both, g_high[...])) + dot(both[:count], g_low[...])
         return image, far
 
+    lane = lax.broadcasted_iota(jnp.int32, (count, LANES), 1)
+    on_diagonal = lane == lax.broadcasted_iota(jnp.int32, (count, LANES), 0)
+
+    def to_row(x):
+        return jnp.sum(jnp.where(on_diagonal, x, 0.0), axis=0, keepdims=True)
+
+    def to_col(x):
+        return jnp.sum(jnp.where(on_diagonal, x, 0.0), axis=1, keepdims=True)
+
     def row_sum(x):
         return jnp.sum(x, axis=1, keepdims=True)
 
     def send_coefs(it, v):
-        coef_out[it, :, :wide] = far_up(v)
-        coef_out[it, :, wide:] = jnp.broadcast_to(row_sum(v * v), (count, LANES))
-        start, finish = spread(coef_out.at[it], coef_in.at[it], c_send.at[it], c_recv.at[it])
-        start()
-        return finish
+        coef_out[it] = far_up(v)
+        return spread(coef_out.at[it], coef_in.at[it], c_send.at[it], c_recv.at[it])
 
     def near_block(l, t, first, columns):
         scale = near_mask[l, t].astype(F32) * (1.0 / leaf)
@@ -243,7 +264,7 @@
             acc = term if acc is None else acc + term
         near_sum[:, across] += scale * acc
 
-    def near(first, v, halos, finish):
+    def near(first, v, halos, finish, between):
         near_sum[...] = jnp.zeros_like(near_sum)
         own = [], []
         for l in range(leaves):
@@ -253,6 +274,10 @@
         both = stacked(v)
         for l, t, m in own[0]:
             near_block(l, t, first, both[:, m * leaf:(m + 1) * leaf])
+            if between:
+                between.pop(0)()
+        for step in between:
+            step()
         finish()
         if first:
             for side in range(2):
@@ -272,26 +297,27 @@
         return jnp.concatenate(diagonal, axis=1) * v + near_sum[...]
 
     def whole_pass(it, v, local, finish_c):
-        sum_out[it] = jnp.broadcast_to(row_sum(v * local), (count, LANES))
+        sum_out[it, :1] = to_row(row_sum(v * local))
+        sum_out[it, 1:] = to_row(row_sum(v * v))
         start, finish = spread(sum_out.at[it], sum_in.at[it], i_send.at[it], i_recv.at[it])
         start()
         finish_c()
-        value = total(coef_out.at[it], coef_in.at[it])
-        s, norm = value[:, :wide], value[:, wide:wide + 1]
+        s = total(coef_out.at[it], coef_in.at[it])
         image, far = far_down(s)
         extra = row_sum(s * image)
         finish()
-        inner = total(sum_out.at[it], sum_in.at[it])[:, :1] + extra
-        return local + far, norm, inner
+        sums = total(sum_out.at[it], sum_in.at[it])
+        return local + far, to_col(sums[1:]), to_col(sums[:1]) + extra
 
     r0 = rhs[...]
-    finish_c = send_coefs(0, r0)
+    start_c, finish_c = send_coefs(0, r0)
 
     def arrived():
         finish_x()
         finish_v()
 
-    local = near(True, r0, halo_v0, arrived)
+    between = [stage(b) for b in range(1, stages + 1)] + [start_c]
+    local = near(True, r0, halo_v0, arrived, between)
     applied0, norm0, inner0 = whole_pass(0, r0, local, finish_c)
     step0 = norm0 / inner0
     r1 = r0 - step0 * applied0
@@ -301,8 +327,9 @@
     start_v, finish_v1 = halo(moved, halo_v1, v_send.at[1], v_recv.at[1])
     start_v()
 
-    finish_c = send_coefs(1, r1)
-    local = near(False, r1, halo_v1, finish_v1)
+    start_c, finish_c = send_coefs(1, r1)
+    start_c()
+    local = near(False, r1, halo_v1, finish_v1, [])
     applied1, norm1, inner1 = whole_pass(1, r1, local, finish_c)
     growth = norm1 / norm0
     step1 = norm1 / (inner1 - growth * norm1 / step0)
@@ -340,12 +367,13 @@
             pltpu.VMEM((wide, points), BF),
             pltpu.VMEM((wide, points), BF),
             pltpu.VMEM((wide, points), BF),
-            pltpu.VMEM((ITERS, count, wide + LANES), F32),
-            pltpu.VMEM((ITERS, peers, count, wide + LANES), F32),
-            pltpu.VMEM((ITERS, count, LANES), F32),
-            pltpu.VMEM((ITERS, peers, count, LANES), F32),
+            pltpu.VMEM((ITERS, count, wide), F32),
+            pltpu.VMEM((ITERS, peers, count, wide), F32),
+            pltpu.VMEM((ITERS, 2, LANES), F32),
+            pltpu.VMEM((ITERS, peers, 2, LANES), F32),
             dma((2,)), dma((2,)), dma((2, 2)), dma((2, 2)),
             dma((ITERS, peers)), dma((ITERS, peers)), dma((ITERS, peers)), dma((ITERS, peers)),
+            pltpu.SemaphoreType.REGULAR((max(n.bit_length() - 1, 1),)),
         ],
         compiler_params=pltpu.CompilerParams(
             collective_id=0, has_side_effects=True, vmem_limit_bytes=60 * 1024 * 1024

time: 36.3 us -> 32.8 us (0.904)
  Pallas kernels: 33.3 us -> 29.8 us
    pallas_call x1, Pallas kernels: 33.3 us -> 29.8 us  [per_device(): pl.pallas_call(functools.partial(kernel, n), out_shape=(jax.ShapeDtypeStr...]
where the time goes in v1:
time: 32.8 us; the launch traced here: 32.6 us
  Pallas kernels  29.8 us (91%)
  local copies, waits for them, and re-layouts  2.14 us (7%)
  between operations  0.65 us (2%)
    pallas_call x1, Pallas kernels, per_device(): pl.pallas_call(functools.partial(kernel, n), out_shape=(jax.ShapeDtypeStr...  29.8 us
    unnamed x4, local copies, waits for them, and re-layouts  2.14 us

profile of v1, /device:TPU:0, one launch (start us, length us, event | category | flops | bytes accessed | tf_op | source)
XLA Modules:
  0.0 32.6 jit_solution(16452023603586066707)
XLA Ops:
  0.6 29.8 %shard_map.95 = (f32[16,1024]{1,0:T(8,128)}, f32[16,1024]{1,0:T(8,128)}) custom-call(f32[8,1024]{1,0:T(8,128)} %coords.1, f32[8,128]{1,0:T(8,128)} %skeleton.1, bf16[2,64,64]{2,1,0:T(8,128)(2,1)} %transfer.1, bf16[256,256]{1,0:T(8,128)(2,1)} %coupling.1, s32[2]{0:T(128)} %parent.1, s32[2,5]{1,0:T(2,128)} %near_mask.1, f32[1,1024]{1,0:T(1,128)} %bitcast.1, ...), custom_call_target="tpu_custom_call" | custom-call | tf_op jit(solution)/shard_map/pallas_call | solution.py:351
  30.5 0.0 copy-start
  30.5 1.5 %copy.12 = f32[16,1024]{1,0:T(8,128)} copy(f32[16,1024]{1,0:T(8,128)} %get-tuple-element.4) | data formatting | bytes 131072
  32.0 0.0 copy-done
  32.0 0.6 %copy.13 = f32[16,1024]{1,0:T(8,128)} copy(f32[16,1024]{1,0:T(8,128)S(1)} %copy-done) | data formatting | bytes 131072
Async XLA Ops:
  30.5 1.5 %copy-start = (f32[16,1024]{1,0:T(8,128)S(1)}, f32[16,1024]{1,0:T(8,128)}, u32[]{:S(2)}) copy-start(f32[16,1024]{1,0:T(8,128)} %get-tuple-element.5) | copy-start | bytes 196612

commit v2 on v1

--- a/solution.py
+++ b/solution.py
@@ -93,6 +93,7 @@
     near_sum, moved, ut_high, ut_low, g_high, g_low,
     coef_out, coef_in, sum_out, sum_in,
     x_send, x_recv, v_send, v_recv, c_send, c_recv, i_send, i_recv, ready,
+    halo_s, halo_t, halo_p, own_t, own_p, gh_high, gh_low, e_send, e_recv,
 ):
     me = lax.axis_index("leaf")
     leaves, slots = near_mask.shape
@@ -175,14 +176,20 @@
 
     @pl.when(me == 0)
     def _():
-        for h in (halo_x, halo_v0, halo_v1):
+        for h in (halo_x, halo_v0, halo_v1, halo_s, halo_t, halo_p):
             h[0] = jnp.zeros(h.shape[1:], F32)
 
     @pl.when(me == n - 1)
     def _():
-        for h in (halo_x, halo_v0, halo_v1):
+        for h in (halo_x, halo_v0, halo_v1, halo_s, halo_t, halo_p):
             h[1] = jnp.zeros(h.shape[1:], F32)
 
+    own_t[...] = transfer[...].astype(F32)
+    parent_row = lax.broadcasted_iota(jnp.int32, (8, LANES), 0)
+    parents = jnp.zeros((8, LANES), F32)
+    for l in range(leaves):
+        parents = jnp.where(parent_row == l, parent[l].astype(F32), parents)
+    own_p[...] = parents
     pl.when(has_other)(lambda: pl.semaphore_wait(barrier, stages + 1))
     pl.when(jnp.logical_not(has_other))(lambda: pl.semaphore_wait(barrier, stages))
     stage(0)()
@@ -190,28 +197,56 @@
     start_v, finish_v = halo(rhs, halo_v0, v_send.at[0], v_recv.at[0])
     start_x()
     start_v()
+    extras = [
+        halo(a, b, e_send.at[i], e_recv.at[i])
+        for i, (a, b) in enumerate(((skeleton, halo_s), (own_t, halo_t), (own_p, halo_p)))
+    ]
+    for start, _ in extras:
+        start()
 
     left, right = features(coords[...])
     left_t[pl.ds(points, points)] = left.T.astype(BF)
     right_f[...] = right.astype(BF)
 
     skeleton_t = features(skeleton[...])[0].T.astype(BF)
+    q = lax.broadcasted_iota(jnp.int32, (wide, rank), 0)
+    q = (q - lax.broadcasted_iota(jnp.int32, (wide, rank), 1)).astype(F32)
+
+    def upward(skel, right, where, weights):
+        bases_t = matern(skel, right)
+        b_high, b_low = split(bases_t * (1.0 / math.sqrt(leaf)))
+        place = jnp.where(q == where * rank, 1.0, 0.0).astype(BF)
+        placed = dot_nt(place, weights).astype(BF)
+        return split(dot(placed, b_high) + dot(placed, b_low))
+
     for l in range(leaves):
         across = pl.ds(l * leaf, leaf)
-        bases_t = matern(skeleton_t[l * rank:(l + 1) * rank], right_f[:, across])
-        b_high, b_low = split(bases_t * (1.0 / math.sqrt(leaf)))
-        q = lax.broadcasted_iota(jnp.int32, (wide, rank), 0)
-        s = lax.broadcasted_iota(jnp.int32, (wide, rank), 1)
-        place = jnp.where(q == s + parent[l] * rank, 1.0, 0.0).astype(BF)
-        placed = dot_nt(place, transfer[l]).astype(BF)
-        ut = dot(placed, b_high) + dot(placed, b_low)
-        u_high, u_low = split(ut)
+        u_high, u_low = upward(
+            skeleton_t[l * rank:(l + 1) * rank], right_f[:, across],
+            parent[l].astype(F32), transfer[l],
+        )
         ut_high[:, across] = u_high
         ut_low[:, across] = u_low
         g = dot(coupling[...], u_high) + dot(coupling[...], u_low)
         g1, g2 = split(g)
         g_high[:, across] = g1
         g_low[:, across] = g2
+
+    def couple_halo():
+        for _, finish in extras:
+            finish()
+        for side in range(2):
+            right = features(halo_x[side])[1].astype(BF)
+            skel = features(halo_s[side])[0].T.astype(BF)
+            for l in range(leaves):
+                across = slice(l * leaf, (l + 1) * leaf)
+                u_high, u_low = upward(
+                    skel[l * rank:(l + 1) * rank], right[:, across],
+                    halo_p[side, l:l + 1, :1], halo_t[side, l].astype(BF),
+                )
+                g1, g2 = split(dot(coupling[...], u_high) + dot(coupling[...], u_low))
+                gh_high[side, :, across] = g1
+                gh_low[side, :, across] = g2
 
     def far_up(v):
         both = stacked(v)
@@ -296,18 +331,19 @@
             diagonal.append(noise[:, l * leaf:(l + 1) * leaf] + ones.astype(F32))
         return jnp.concatenate(diagonal, axis=1) * v + near_sum[...]
 
-    def whole_pass(it, v, local, finish_c):
+    def whole_pass(it, v, local, finish_c, during):
         sum_out[it, :1] = to_row(row_sum(v * local))
         sum_out[it, 1:] = to_row(row_sum(v * v))
         start, finish = spread(sum_out.at[it], sum_in.at[it], i_send.at[it], i_recv.at[it])
         start()
+        during()
         finish_c()
         s = total(coef_out.at[it], coef_in.at[it])
         image, far = far_down(s)
         extra = row_sum(s * image)
         finish()
         sums = total(sum_out.at[it], sum_in.at[it])
-        return local + far, to_col(sums[1:]), to_col(sums[:1]) + extra
+        return local + far, to_col(sums[1:]), to_col(sums[:1]) + extra, s
 
     r0 = rhs[...]
     start_c, finish_c = send_coefs(0, r0)
@@ -318,19 +354,30 @@
 
     between = [stage(b) for b in range(1, stages + 1)] + [start_c]
     local = near(True, r0, halo_v0, arrived, between)
-    applied0, norm0, inner0 = whole_pass(0, r0, local, finish_c)
+    moved[...] = local
+    start_v, finish_v1 = halo(moved, halo_v1, v_send.at[1], v_recv.at[1])
+
+    def during():
+        start_v()
+        couple_halo()
+
+    applied0, norm0, inner0, s0 = whole_pass(0, r0, local, finish_c, during)
     step0 = norm0 / inner0
     r1 = r0 - step0 * applied0
-    moved[...] = r1
     solution_ref[...] = step0 * r0
     residual_ref[...] = applied0
-    start_v, finish_v1 = halo(moved, halo_v1, v_send.at[1], v_recv.at[1])
-    start_v()
 
     start_c, finish_c = send_coefs(1, r1)
     start_c()
-    local = near(False, r1, halo_v1, finish_v1, [])
-    applied1, norm1, inner1 = whole_pass(1, r1, local, finish_c)
+
+    finish_v1()
+    both0 = stacked(s0)
+    moved_in = []
+    for side in range(2):
+        far = folded(dot(both0, gh_high[side])) + dot(both0[:count], gh_low[side])
+        moved_in.append(halo_v0[side] - step0 * (halo_v1[side] + far))
+    local = near(False, r1, moved_in, lambda: None, [])
+    applied1, norm1, inner1, _ = whole_pass(1, r1, local, finish_c, lambda: None)
     growth = norm1 / norm0
     step1 = norm1 / (inner1 - growth * norm1 / step0)
     solution_ref[...] = solution_ref[...] + step1 * (r1 + growth * rhs[...])
@@ -374,6 +421,14 @@
             dma((2,)), dma((2,)), dma((2, 2)), dma((2, 2)),
             dma((ITERS, peers)), dma((ITERS, peers)), dma((ITERS, peers)), dma((ITERS, peers)),
             pltpu.SemaphoreType.REGULAR((max(n.bit_length() - 1, 1),)),
+            pltpu.VMEM((2,) + skeleton.shape, F32),
+            pltpu.VMEM((2,) + transfer.shape, F32),
+            pltpu.VMEM((2, 8, LANES), F32),
+            pltpu.VMEM(transfer.shape, F32),
+            pltpu.VMEM((8, LANES), F32),
+            pltpu.VMEM((2, wide, points), BF),
+            pltpu.VMEM((2, wide, points), BF),
+            dma((3, 2)), dma((3, 2)),
         ],
         compiler_params=pltpu.CompilerParams(
             collective_id=0, has_side_effects=True, vmem_limit_bytes=60 * 1024 * 1024

time: 32.8 us -> 32.4 us (0.988)
    pallas_call x1, Pallas kernels: 29.8 us -> 29.5 us  [per_device(): pl.pallas_call(functools.partial(kernel, n), out_shape=(jax.ShapeDtypeStr...]
where the time goes in v2:
time: 32.4 us; the launch traced here: 32.3 us
  Pallas kernels  29.5 us (91%)
  local copies, waits for them, and re-layouts  2.14 us (7%)
  between operations  0.65 us (2%)
    pallas_call x1, Pallas kernels, per_device(): pl.pallas_call(functools.partial(kernel, n), out_shape=(jax.ShapeDtypeStr...  29.5 us
    unnamed x4, local copies, waits for them, and re-layouts  2.14 us

profile of v2, /device:TPU:0, one launch (start us, length us, event | category | flops | bytes accessed | tf_op | source)
XLA Modules:
  0.0 32.3 jit_solution(7582251332722043234)
XLA Ops:
  0.6 29.5 %shard_map.95 = (f32[16,1024]{1,0:T(8,128)}, f32[16,1024]{1,0:T(8,128)}) custom-call(f32[8,1024]{1,0:T(8,128)} %coords.1, f32[8,128]{1,0:T(8,128)} %skeleton.1, bf16[2,64,64]{2,1,0:T(8,128)(2,1)} %transfer.1, bf16[256,256]{1,0:T(8,128)(2,1)} %coupling.1, s32[2]{0:T(128)} %parent.1, s32[2,5]{1,0:T(2,128)} %near_mask.1, f32[1,1024]{1,0:T(1,128)} %bitcast.1, ...), custom_call_target="tpu_custom_call" | custom-call | tf_op jit(solution)/shard_map/pallas_call | solution.py:398
  30.1 0.0 copy-start
  30.1 1.5 %copy.12 = f32[16,1024]{1,0:T(8,128)} copy(f32[16,1024]{1,0:T(8,128)} %get-tuple-element.4) | data formatting | bytes 131072
  31.6 0.0 copy-done
  31.6 0.6 %copy.13 = f32[16,1024]{1,0:T(8,128)} copy(f32[16,1024]{1,0:T(8,128)S(1)} %copy-done) | data formatting | bytes 131072
Async XLA Ops:
  30.1 1.5 %copy-start = (f32[16,1024]{1,0:T(8,128)S(1)}, f32[16,1024]{1,0:T(8,128)}, u32[]{:S(2)}) copy-start(f32[16,1024]{1,0:T(8,128)} %get-tuple-element.5) | copy-start | bytes 196612
